TPU v7x, 32 devices: a whole 2x2x4 slice. The times are simulated.
32 devices in a mesh: section: 2 (over core), hid: 8 (over z, x), mod: 2 (over y).
Axes of the slice: x: 2, y: 2, z: 4, core: 2. Of those that a mesh axis runs over, the one named last changes fastest.
Arguments:
- tokens: float32 [2048, 5120], P(('section', 'hid'), 'mod'), may hold values from -200 to 200
- gain_first: float32 [5120], P('mod'), may hold values from 0.1 to 1.9
- gate_first: bfloat16 [5120, 13824], P('mod', 'hid'), may hold values from -0.078125 to 0.078125
- up_first: bfloat16 [5120, 13824], P('mod', 'hid'), may hold values from -0.078125 to 0.078125
- down_first: bfloat16 [13824, 5120], P('hid', 'mod'), may hold values from -0.0546875 to 0.0546875
- gain_second: float32 [5120], P('mod'), may hold values from 0.1 to 1.9
- gate_second: bfloat16 [5120, 13824], P('mod', ('section', 'hid')), may hold values from -0.078125 to 0.078125
- up_second: bfloat16 [5120, 13824], P('mod', ('section', 'hid')), may hold values from -0.078125 to 0.078125
- down_second: bfloat16 [13824, 5120], P(('section', 'hid'), 'mod'), may hold values from -0.0546875 to 0.0546875
Outputs:
- result: float32 [2048, 5120], P(('section', 'hid'), 'mod')
All inputs are finite; a program needn't handle non-finite values.
Results may differ from a plain program's by a relative error of at most 0.006.
Values may be sent and summed in bfloat16 or wider, within the bound.
A program may use at most 128 MiB of HBM per device.

v0:
```python
import jax
import jax.numpy as jnp
from jax import lax
from jax.sharding import PartitionSpec as P

D = 5120
epsilon = 1e-06


def scale_rows(stream, square_sum, gain):
    return (stream * lax.rsqrt(square_sum[:, None] / D + epsilon) * gain).astype(jnp.bfloat16)


def both_products(segment, w_gate, w_up):
    gate_part = jnp.dot(segment, w_gate, preferred_element_type=jnp.float32).astype(jnp.bfloat16)
    up_part = jnp.dot(segment, w_up, preferred_element_type=jnp.float32).astype(jnp.bfloat16)
    return jnp.concatenate([gate_part, up_part], axis=1)


def swiglu(summed, hidden_units):
    return (jax.nn.silu(summed[:, :hidden_units]) * summed[:, hidden_units:]).astype(jnp.bfloat16)


def per_device(
    tokens,
    gain_first,
    gate_first,
    up_first,
    down_first,
    gain_second,
    gate_second,
    up_second,
    down_second,
):
    square_first = lax.psum(jnp.sum(tokens * tokens, axis=1), "mod")
    normed_first = scale_rows(tokens, square_first, gain_first)
    partial_first = both_products(
        lax.all_gather(normed_first, "hid", axis=0, tiled=True), gate_first, up_first
    )
    units_first = gate_first.shape[1]
    summed_first = lax.psum_scatter(
        partial_first.astype(jnp.float32).astype(jnp.bfloat16),
        "mod",
        scatter_dimension=0,
        tiled=True,
    ).astype(jnp.float32)
    activated_first = swiglu(summed_first, units_first)
    terms_first = jnp.dot(
        lax.all_gather(activated_first, "mod", axis=0, tiled=True),
        down_first,
        preferred_element_type=jnp.float32,
    )
    middle = tokens + lax.psum_scatter(
        terms_first.astype(jnp.bfloat16), "hid", scatter_dimension=0, tiled=True
    ).astype(jnp.float32)
    square_second = lax.psum(jnp.sum(middle * middle, axis=1), "mod")
    normed_second = scale_rows(middle, square_second, gain_second)
    partial_second = both_products(
        lax.all_gather(normed_second, ("section", "hid"), axis=0, tiled=True),
        gate_second,
        up_second,
    )
    units_second = gate_second.shape[1]
    summed_second = lax.psum_scatter(
        partial_second.astype(jnp.float32).astype(jnp.bfloat16),
        "mod",
        scatter_dimension=0,
        tiled=True,
    ).astype(jnp.float32)
    activated_second = swiglu(summed_second, units_second)
    terms_second = jnp.dot(
        lax.all_gather(activated_second, "mod", axis=0, tiled=True),
        down_second,
        preferred_element_type=jnp.float32,
    )
    return middle + lax.psum_scatter(
        terms_second.astype(jnp.bfloat16), ("section", "hid"), scatter_dimension=0, tiled=True
    ).astype(jnp.float32)


def solution(mesh):
    in_specs = (
        P(("section", "hid"), "mod"),
        P("mod"),
        P("mod", "hid"),
        P("mod", "hid"),
        P("hid", "mod"),
        P("mod"),
        P("mod", ("section", "hid")),
        P("mod", ("section", "hid")),
        P(("section", "hid"), "mod"),
    )
    out_specs = P(("section", "hid"), "mod")
    return jax.shard_map(
        per_device, mesh=mesh, in_specs=in_specs, out_specs=out_specs, check_vma=False
    )
```

profile of v0, /device:TPU:0, one launch (start us, length us, event | category | flops | bytes accessed | tf_op | source)
XLA Modules:
  0.0 806.3 jit_solution(4746414149843503871)
XLA Ops:
  6.5 0.0 all-gather.5.cloned.1.call-start
  6.5 1.5 multiply_reduce_fusion.1
  8.0 5.9 psum.14
  13.9 2.3 multiply_convert_fusion.1
  16.3 0.0 all-gather.5.cloned.1.call-update
  16.3 0.0 reduce-scatter.5.cloned.1.call-start
  16.3 87.7 %all-gather.5.cloned.1.call-done = bf16[1024,2560]{1,0:T(8,128)(2,1)} async-done(((bf16[128,2560]{1,0:T(8,128)(2,1)}), bf16[1024,2560]{1,0:T(8,128)(2,1)}) %all-gather.5.cloned.1.call-update) | async-done | bytes 5242896 | tf_op jit(solution)/shard_map/all_gather | solution.py:38
  104.1 0.0 copy-start.4
  104.1 14.3 %convolution_convert_fusion.2 = bf16[1024,1728]{0,1:T(8,128)(2,1)S(1)} fusion(bf16[1024,2560]{1,0:T(8,128)(2,1)} %all-gather.5.cloned.1.call-done, bf16[2560,1728]{0,1:T(8,128)(2,1)} %param.12), kind=kOutput, calls=%fused_computation.4 | convolution fusion | flops 9061466112 | bytes 17629184 | tf_op jit(solution)/shard_map/dot_general | solution.py:16
  118.4 0.0 copy-done.4
  118.4 13.0 %convolution_convert_fusion.3 = bf16[1024,1728]{0,1:T(8,128)(2,1)} fusion(bf16[1024,2560]{1,0:T(8,128)(2,1)S(1)} %copy-done.4, bf16[2560,1728]{0,1:T(8,128)(2,1)} %param.11), kind=kOutput, calls=%fused_computation.5 | convolution fusion | flops 9061466112 | bytes 17629184 | tf_op jit(solution)/shard_map/dot_general | solution.py:15
  131.4 5.7 pad_maximum_fusion
  137.1 0.0 reduce-scatter.5.cloned.1.call-update
  137.2 0.0 all-gather.7.cloned.1.call-start
  137.2 84.0 %reduce-scatter.5.cloned.1.call-done = bf16[512,3456]{0,1:T(8,128)(2,1)} async-done(((bf16[1024,3456]{0,1:T(8,128)(2,1)}), bf16[512,3456]{0,1:T(8,128)(2,1)}) %reduce-scatter.5.cloned.1.call-update) | async-done | bytes 3538960 | tf_op jit(solution)/shard_map/reduce_scatter | solution.py:41
  221.2 3.0 convert_element_type.49
  224.2 2.5 fusion.1
  226.7 0.0 all-gather.7.cloned.1.call-update
  226.7 0.2 reduce-scatter.7.cloned.1.call-start
  226.9 49.3 %all-gather.7.cloned.1.call-done = bf16[1024,1728]{0,1:T(8,128)(2,1)} async-done(((bf16[512,1728]{0,1:T(8,128)(2,1)}), bf16[1024,1728]{0,1:T(8,128)(2,1)}) %all-gather.7.cloned.1.call-update) | async-done | bytes 3538960 | tf_op jit(solution)/shard_map/all_gather | solution.py:49
  276.2 15.0 %convolution_convert_fusion.1 = bf16[1024,2560]{1,0:T(8,128)(2,1)} fusion(bf16[1024,1728]{0,1:T(8,128)(2,1)} %all-gather.7.cloned.1.call-done, bf16[1728,2560]{1,0:T(8,128)(2,1)} %param.13), kind=kOutput, calls=%fused_computation.3 | convolution fusion | flops 9062318080 | bytes 17629184 | tf_op jit(solution)/shard_map/dot_general | solution.py:48
  291.2 0.0 copy-start
  291.2 0.0 copy-start.2
  291.2 0.0 reduce-scatter.7.cloned.1.call-update
  291.2 0.0 all-gather.9.cloned.1.call-start
  291.3 103.1 %reduce-scatter.7.cloned.1.call-done = bf16[128,2560]{1,0:T(8,128)(2,1)} async-done(((bf16[1024,2560]{1,0:T(8,128)(2,1)}), bf16[128,2560]{1,0:T(8,128)(2,1)}) %reduce-scatter.7.cloned.1.call-update) | async-done | bytes 655376 | tf_op jit(solution)/shard_map/reduce_scatter | solution.py:53
  394.3 0.0 copy-done
  394.3 1.3 multiply_reduce_fusion
  395.7 4.9 psum.15
  400.6 0.0 copy-done.2
  400.6 2.1 multiply_convert_fusion
  402.8 0.0 all-gather.9.cloned.1.call-update
  402.8 0.0 reduce-scatter.9.cloned.1.call-start
  402.8 87.3 %all-gather.9.cloned.1.call-done = bf16[2048,2560]{1,0:T(8,128)(2,1)} async-done(((bf16[128,2560]{1,0:T(8,128)(2,1)}), bf16[2048,2560]{1,0:T(8,128)(2,1)}) %all-gather.9.cloned.1.call-update) | async-done | bytes 10485776 | tf_op jit(solution)/shard_map/all_gather | solution.py:59
  490.1 0.0 copy-start.3
  490.1 13.5 %convolution_convert_fusion.4 = bf16[2048,864]{0,1:T(8,128)(2,1)S(1)} fusion(bf16[2048,2560]{1,0:T(8,128)(2,1)} %all-gather.9.cloned.1.call-done, bf16[2560,864]{0,1:T(8,128)(2,1)} %param.16), kind=kOutput, calls=%fused_computation.10 | convolution fusion | flops 9061466112 | bytes 18448384 | tf_op jit(solution)/shard_map/dot_general | solution.py:16
  503.6 0.0 copy-done.3
  503.6 12.5 %convolution_convert_fusion.5 = bf16[2048,864]{0,1:T(8,128)(2,1)} fusion(bf16[2048,2560]{1,0:T(8,128)(2,1)S(1)} %copy-done.3, bf16[2560,864]{0,1:T(8,128)(2,1)} %param.15), kind=kOutput, calls=%fused_computation.11 | convolution fusion | flops 9061466112 | bytes 18448384 | tf_op jit(solution)/shard_map/dot_general | solution.py:15
  516.1 6.0 pad_maximum_fusion.1
  522.1 0.0 reduce-scatter.9.cloned.1.call-update
  522.1 0.3 all-gather.11.cloned.1.call-start
  522.4 83.8 %reduce-scatter.9.cloned.1.call-done = bf16[1024,1728]{0,1:T(8,128)(2,1)} async-done(((bf16[2048,1728]{0,1:T(8,128)(2,1)}), bf16[1024,1728]{0,1:T(8,128)(2,1)}) %reduce-scatter.9.cloned.1.call-update) | async-done | bytes 3538960 | tf_op jit(solution)/shard_map/reduce_scatter | solution.py:64
  606.2 2.8 convert_element_type.56
  609.1 2.4 fusion
  611.5 0.0 all-gather.11.cloned.1.call-update
  611.5 0.0 reduce-scatter.11.cloned.1.call-start
  611.5 49.4 %all-gather.11.cloned.1.call-done = bf16[2048,864]{0,1:T(8,128)(2,1)} async-done(((bf16[1024,864]{0,1:T(8,128)(2,1)}), bf16[2048,864]{0,1:T(8,128)(2,1)}) %all-gather.11.cloned.1.call-update) | async-done | bytes 3538960 | tf_op jit(solution)/shard_map/all_gather | solution.py:72
  661.0 16.5 %convolution_convert_fusion = bf16[2048,2560]{1,0:T(8,128)(2,1)} fusion(bf16[2048,864]{0,1:T(8,128)(2,1)} %all-gather.11.cloned.1.call-done, bf16[864,2560]{1,0:T(8,128)(2,1)} %param.17), kind=kOutput, calls=%fused_computation | convolution fusion | flops 9064939520 | bytes 18448384 | tf_op jit(solution)/shard_map/dot_general | solution.py:71
  677.5 0.0 copy-start.1
  677.5 0.0 reduce-scatter.11.cloned.1.call-update
  677.6 119.6 %reduce-scatter.11.cloned.1.call-done = bf16[128,2560]{1,0:T(8,128)(2,1)} async-done(((bf16[2048,2560]{1,0:T(8,128)(2,1)}), bf16[128,2560]{1,0:T(8,128)(2,1)}) %reduce-scatter.11.cloned.1.call-update) | async-done | bytes 655376 | tf_op jit(solution)/shard_map/reduce_scatter | solution.py:76
  797.2 0.0 copy-done.1
  797.2 2.3 convert_add_fusion
  (2 shorter events, 0.0 us)
Async XLA Ops:
  6.5 97.5 %all-gather.5.cloned.1.call-start = ((), (), s32[]{:S(2)}) async-start(), calls=%async_computation.4 | async-start | bytes 5898240 | tf_op jit(solution)/shard_map/all_gather | solution.py:38
  16.3 204.9 %reduce-scatter.5.cloned.1.call-start = ((), (), s32[]{:S(2)}) async-start(), calls=%async_computation.5 | async-start | bytes 10616832 | tf_op jit(solution)/shard_map/reduce_scatter | solution.py:41
  104.1 14.3 %copy-start.4 = (bf16[1024,2560]{1,0:T(8,128)(2,1)S(1)}, bf16[1024,2560]{1,0:T(8,128)(2,1)}, u32[]{:S(2)}) copy-start(bf16[1024,2560]{1,0:T(8,128)(2,1)} %all-gather.5.cloned.1.call-done) | copy-start | bytes 15728644
  137.2 139.0 %all-gather.7.cloned.1.call-start = ((), (), s32[]{:S(2)}) async-start(), calls=%async_computation.6 | async-start | bytes 5308416 | tf_op jit(solution)/shard_map/all_gather | solution.py:49
  226.7 167.6 %reduce-scatter.7.cloned.1.call-start = ((), (), s32[]{:S(2)}) async-start(), calls=%async_computation.7 | async-start | bytes 5898240 | tf_op jit(solution)/shard_map/reduce_scatter | solution.py:53
  291.2 103.2 %copy-start = (f32[128,2560]{1,0:T(8,128)S(1)}, f32[128,2560]{1,0:T(8,128)}, u32[]{:S(2)}) copy-start(f32[128,2560]{1,0:T(8,128)} %param.9) | copy-start | bytes 3932164
  291.2 109.4 %copy-start.2 = (f32[2560]{0:T(1024)S(1)}, f32[2560]{0:T(1024)}, u32[]{:S(2)}) copy-start(f32[2560]{0:T(1024)} %param.14) | copy-start | bytes 30724
  291.2 198.9 %all-gather.9.cloned.1.call-start = ((), (), s32[]{:S(2)}) async-start(), calls=%async_computation.8 | async-start | bytes 11141120 | tf_op jit(solution)/shard_map/all_gather | solution.py:59
  402.8 203.4 %reduce-scatter.9.cloned.1.call-start = ((), (), s32[]{:S(2)}) async-start(), calls=%async_computation.9 | async-start | bytes 10616832 | tf_op jit(solution)/shard_map/reduce_scatter | solution.py:64
  490.1 13.5 %copy-start.3 = (bf16[2048,2560]{1,0:T(8,128)(2,1)S(1)}, bf16[2048,2560]{1,0:T(8,128)(2,1)}, u32[]{:S(2)}) copy-start(bf16[2048,2560]{1,0:T(8,128)(2,1)} %all-gather.9.cloned.1.call-done) | copy-start | bytes 31457284
  522.1 138.9 %all-gather.11.cloned.1.call-start = ((), (), s32[]{:S(2)}) async-start(), calls=%async_computation.10 | async-start | bytes 5308416 | tf_op jit(solution)/shard_map/all_gather | solution.py:72
  611.5 185.7 %reduce-scatter.11.cloned.1.call-start = ((), (), s32[]{:S(2)}) async-start(), calls=%async_computation.11 | async-start | bytes 11141120 | tf_op jit(solution)/shard_map/reduce_scatter | solution.py:76
  677.5 119.6 %copy-start.1 = (bf16[128,2560]{1,0:T(8,128)(2,1)S(1)}, bf16[128,2560]{1,0:T(8,128)(2,1)}, u32[]{:S(2)}) copy-start(bf16[128,2560]{1,0:T(8,128)(2,1)} %reduce-scatter.7.cloned.1.call-done) | copy-start | bytes 1966084
Sparse Core Ops, SparseCore 0:
  16.4 87.6 all-gather.4
  137.3 83.8 reduce-scatter.4
  226.8 49.3 all-gather.6
  291.3 102.9 reduce-scatter.6
  402.9 87.1 all-gather.8
  522.2 83.9 reduce-scatter.8
  611.6 49.3 all-gather.10
  677.7 119.4 reduce-scatter.10
where the time goes:
time: 807 us; the launch traced here: 806 us
  waiting for transfers between devices  664 us (82%)
  matrix products  84.8 us (11%)
  other arithmetic  32.1 us (4%)
  between operations  13.6 us (2%)
  blocking collectives  10.8 us (1%)
    reduce_scatter x1, waiting for transfers between devices, per_device(): lax.psum_scatter(terms_second.astype(jnp.bfloat16), ('section', 'hid'), s...  120 us
    reduce_scatter x1, waiting for transfers between devices, per_device(): lax.psum_scatter(terms_first.astype(jnp.bfloat16), 'hid', scatter_dimensi...  103 us
    all_gather x1, waiting for transfers between devices, per_device(): lax.all_gather(normed_first, 'hid', axis=0, tiled=True)  87.7 us
    all_gather x1, waiting for transfers between devices, per_device(): lax.all_gather(normed_second, ('section', 'hid'), axis=0, tiled=True)  87.3 us
    reduce_scatter x1, waiting for transfers between devices, per_device(): lax.psum_scatter(partial_first.astype(jnp.float32).astype(jnp.bfloat16),...  84 us
    reduce_scatter x1, waiting for transfers between devices, per_device(): lax.psum_scatter(partial_second.astype(jnp.float32).astype(jnp.bfloat16),...  83.8 us
    all_gather x1, waiting for transfers between devices, per_device(): lax.all_gather(activated_second, 'mod', axis=0, tiled=True)  49.4 us
    all_gather x1, waiting for transfers between devices, per_device(): lax.all_gather(activated_first, 'mod', axis=0, tiled=True)  49.3 us
  transfers between devices with their start and end apart: 8, of which 8 were waited for; matrix products, arithmetic and copies ran while one was open for 0% of the time, Pallas kernels for 0%

commit v1 on v0

--- a/solution.py
+++ b/solution.py
@@ -5,6 +5,28 @@
 
 D = 5120
 epsilon = 1e-06
+
+
+def joined_along(blocks, dim):
+    shape = list(blocks.shape[1:])
+    shape[dim] *= blocks.shape[0]
+    return jnp.moveaxis(blocks, 0, dim).reshape(shape)
+
+
+def doubled(x, axis):
+    peers = lax.axis_size(axis)
+    blocks = x[None]
+    for level in range(peers.bit_length() - 1):
+        bit = 1 << level
+        other = lax.ppermute(blocks, axis, [(i, i ^ bit) for i in range(peers)])
+        both = jnp.stack([blocks, other])
+        upper = lax.axis_index(axis) >> level & 1
+        blocks = jnp.where(upper == 0, both, both[::-1]).reshape(-1, *x.shape)
+    return blocks
+
+
+def collect(x, axis, dim):
+    return joined_along(doubled(x, axis), dim)
 
 
 def scale_rows(stream, square_sum, gain):
@@ -34,9 +56,7 @@
 ):
     square_first = lax.psum(jnp.sum(tokens * tokens, axis=1), "mod")
     normed_first = scale_rows(tokens, square_first, gain_first)
-    partial_first = both_products(
-        lax.all_gather(normed_first, "hid", axis=0, tiled=True), gate_first, up_first
-    )
+    partial_first = both_products(collect(normed_first, "hid", 0), gate_first, up_first)
     units_first = gate_first.shape[1]
     summed_first = lax.psum_scatter(
         partial_first.astype(jnp.float32).astype(jnp.bfloat16),

time: 807 us -> 882 us (1.093)
  waiting for transfers between devices: 664 us -> 731 us
    ppermute x0 -> x3, waiting for transfers between devices: none -> 151 us  [doubled(): other = lax.ppermute(blocks, axis, [(i, i ^ bit) for i in range(peers)])]
    all_gather x1 -> x0, waiting for transfers between devices: 87.7 us -> none  [per_device(): lax.all_gather(normed_first, 'hid', axis=0, tiled=True)]
  transfers between devices with their start and end apart: 8 -> 10, of which waited for: 8 -> 10; matrix products, arithmetic and copies ran while one was open for 0% -> 0% of each run, Pallas kernels for 0% -> 0%
where the time goes in v1:
time: 882 us
  waiting for transfers between devices  731 us (83%)
  matrix products  81.5 us (9%)
  other arithmetic  37.9 us (4%)
  between operations  13.6 us (2%)
  blocking collectives  10.8 us (1%)
    ppermute x3, waiting for transfers between devices, doubled(): other = lax.ppermute(blocks, axis, [(i, i ^ bit) for i in range(peers)])  151 us
    reduce_scatter x1, waiting for transfers between devices, per_device(): lax.psum_scatter(terms_second.astype(jnp.bfloat16), ('section', 'hid'), s...  120 us
    reduce_scatter x1, waiting for transfers between devices, per_device(): lax.psum_scatter(terms_first.astype(jnp.bfloat16), 'hid', scatter_dimensi...  103 us
    all_gather x1, waiting for transfers between devices, per_device(): lax.all_gather(normed_second, ('section', 'hid'), axis=0, tiled=True)  87.3 us
    reduce_scatter x1, waiting for transfers between devices, per_device(): lax.psum_scatter(partial_first.astype(jnp.float32).astype(jnp.bfloat16),...  86.6 us
    reduce_scatter x1, waiting for transfers between devices, per_device(): lax.psum_scatter(partial_second.astype(jnp.float32).astype(jnp.bfloat16),...  83.8 us
    all_gather x1, waiting for transfers between devices, per_device(): lax.all_gather(activated_second, 'mod', axis=0, tiled=True)  49.5 us
    all_gather x1, waiting for transfers between devices, per_device(): lax.all_gather(activated_first, 'mod', axis=0, tiled=True)  49.3 us
  transfers between devices with their start and end apart: 10, of which 10 were waited for; matrix products, arithmetic and copies ran while one was open for 0% of the time, Pallas kernels for 0%

profile of v1, /device:TPU:0, one launch (start us, length us, event | category | flops | bytes accessed | tf_op | source)
XLA Modules:
  0.0 881.7 jit_solution(5033510767490989031)
XLA Ops:
  6.5 0.0 reduce-scatter.5.cloned.1.call-start
  6.5 1.5 multiply_reduce_fusion.1
  8.0 5.9 psum.14
  13.9 1.5 fusion.5
  15.5 2.1 collective-permute-start
  17.5 13.6 %collective-permute-done = bf16[1,128,2560]{2,1,0:T(8,128)(2,1)S(1)} collective-permute-done((bf16[1,128,2560]{2,1,0:T(8,128)(2,1)S(1)}, bf16[1,128,2560]{2,1,0:T(8,128)(2,1)S(1)}, u32[]{:S(2)}, u32[]{:S(2)}) %collective-permute-start) | collective-permute-done | bytes 655392 | tf_op jit(solution)/shard_map/ppermute | solution.py:21
  31.1 0.1 pad_maximum_fusion.4
  31.3 1.3 fusion.3
  32.6 1.8 collective-permute-start.1
  34.4 27.2 %collective-permute-done.1 = bf16[2,128,2560]{2,1,0:T(8,128)(2,1)S(1)} collective-permute-done((bf16[2,128,2560]{2,1,0:T(8,128)(2,1)}, bf16[2,128,2560]{2,1,0:T(8,128)(2,1)S(1)}, u32[]{:S(2)}, u32[]{:S(2)}) %collective-permute-start.1) | collective-permute-done | bytes 1310752 | tf_op jit(solution)/shard_map/ppermute | solution.py:21
  61.6 0.2 pad_maximum_fusion.3
  61.8 0.4 reverse_select_fusion.1
  62.3 2.6 collective-permute-start.2
  64.9 110.7 %collective-permute-done.2 = bf16[4,128,2560]{2,1,0:T(8,128)(2,1)} collective-permute-done((bf16[4,128,2560]{2,1,0:T(8,128)(2,1)S(1)}, bf16[4,128,2560]{2,1,0:T(8,128)(2,1)}, u32[]{:S(2)}, u32[]{:S(2)}) %collective-permute-start.2) | collective-permute-done | bytes 2621472 | tf_op jit(solution)/shard_map/ppermute | solution.py:21
  175.5 2.2 pad_maximum_fusion.2
  177.8 0.0 slice-start
  177.8 1.1 reverse_select_fusion
  178.8 0.0 slice-start.1
  178.9 0.0 slice-start.2
  178.9 12.0 %convolution_convert_fusion.2 = bf16[1024,1728]{0,1:T(8,128)(2,1)S(1)} fusion(bf16[1024,2560]{1,0:T(8,128)(2,1)S(1)} %bitcast.28, bf16[2560,1728]{0,1:T(8,128)(2,1)} %param.12), kind=kOutput, calls=%fused_computation.7 | convolution fusion | flops 9061466112 | bytes 17629184 | tf_op jit(solution)/shard_map/dot_general | solution.py:38
  190.8 0.0 slice-done
  190.8 0.0 slice-done.1
  190.8 0.0 slice-done.2
  190.9 10.8 %convolution_convert_fusion.3 = bf16[1024,1728]{0,1:T(8,128)(2,1)} fusion(bf16[1024,2560]{1,0:T(8,128)(2,1)S(1)} %bitcast.29, bf16[2560,1728]{0,1:T(8,128)(2,1)S(1)} %bitcast.33), kind=kOutput, calls=%fused_computation.8 | convolution fusion | flops 9061466112 | bytes 17629184 | tf_op jit(solution)/shard_map/dot_general | solution.py:37
  201.6 5.7 pad_maximum_fusion
  207.4 0.0 reduce-scatter.5.cloned.1.call-update
  207.4 0.0 all-gather.4.cloned.1.call-start
  207.4 86.6 %reduce-scatter.5.cloned.1.call-done = bf16[512,3456]{0,1:T(8,128)(2,1)} async-done(((bf16[1024,3456]{0,1:T(8,128)(2,1)}), bf16[512,3456]{0,1:T(8,128)(2,1)}) %reduce-scatter.5.cloned.1.call-update) | async-done | bytes 3538960 | tf_op jit(solution)/shard_map/reduce_scatter | solution.py:61
  294.0 3.0 convert_element_type.49
  297.0 2.5 fusion.1
  299.4 0.0 all-gather.4.cloned.1.call-update
  299.5 0.2 reduce-scatter.7.cloned.1.call-start
  299.7 49.3 %all-gather.4.cloned.1.call-done = bf16[1024,1728]{0,1:T(8,128)(2,1)} async-done(((bf16[512,1728]{0,1:T(8,128)(2,1)}), bf16[1024,1728]{0,1:T(8,128)(2,1)}) %all-gather.4.cloned.1.call-update) | async-done | bytes 3538960 | tf_op jit(solution)/shard_map/all_gather | solution.py:69
  349.0 15.0 %convolution_convert_fusion.1 = bf16[1024,2560]{1,0:T(8,128)(2,1)} fusion(bf16[1024,1728]{0,1:T(8,128)(2,1)} %all-gather.4.cloned.1.call-done, bf16[1728,2560]{1,0:T(8,128)(2,1)} %param.13), kind=kOutput, calls=%fused_computation.4 | convolution fusion | flops 9062318080 | bytes 17629184 | tf_op jit(solution)/shard_map/dot_general | solution.py:68
  364.0 0.0 copy-start
  364.0 0.0 copy-start.2
  364.0 0.0 reduce-scatter.7.cloned.1.call-update
  364.0 0.0 all-gather.6.cloned.1.call-start
  364.1 103.1 %reduce-scatter.7.cloned.1.call-done = bf16[128,2560]{1,0:T(8,128)(2,1)} async-done(((bf16[1024,2560]{1,0:T(8,128)(2,1)}), bf16[128,2560]{1,0:T(8,128)(2,1)}) %reduce-scatter.7.cloned.1.call-update) | async-done | bytes 655376 | tf_op jit(solution)/shard_map/reduce_scatter | solution.py:73
  467.2 0.0 copy-done
  467.2 1.3 multiply_reduce_fusion
  468.5 4.9 psum.15
  473.5 0.0 copy-done.2
  473.5 2.1 multiply_convert_fusion
  475.6 0.0 all-gather.6.cloned.1.call-update
  475.6 0.0 reduce-scatter.9.cloned.1.call-start
  475.7 87.3 %all-gather.6.cloned.1.call-done = bf16[2048,2560]{1,0:T(8,128)(2,1)} async-done(((bf16[128,2560]{1,0:T(8,128)(2,1)}), bf16[2048,2560]{1,0:T(8,128)(2,1)}) %all-gather.6.cloned.1.call-update) | async-done | bytes 10485776 | tf_op jit(solution)/shard_map/all_gather | solution.py:79
  562.9 14.8 %convolution_convert_fusion.4 = bf16[2048,864]{0,1:T(8,128)(2,1)} fusion(bf16[2048,2560]{1,0:T(8,128)(2,1)} %all-gather.6.cloned.1.call-done, bf16[2560,864]{0,1:T(8,128)(2,1)} %param.16), kind=kOutput, calls=%fused_computation.13 | convolution fusion | flops 9061466112 | bytes 18448384 | tf_op jit(solution)/shard_map/dot_general | solution.py:38
  577.7 0.0 copy-done.3
  577.7 12.4 %convolution_convert_fusion.5 = bf16[2048,864]{0,1:T(8,128)(2,1)} fusion(bf16[2048,2560]{1,0:T(8,128)(2,1)S(1)} %copy-done.3, bf16[2560,864]{0,1:T(8,128)(2,1)} %param.15), kind=kOutput, calls=%fused_computation.14 | convolution fusion | flops 9061466112 | bytes 18448384 | tf_op jit(solution)/shard_map/dot_general | solution.py:37
  590.1 7.3 pad_maximum_fusion.1
  597.5 0.0 reduce-scatter.9.cloned.1.call-update
  597.5 0.3 all-gather.8.cloned.1.call-start
  597.7 83.8 %reduce-scatter.9.cloned.1.call-done = bf16[1024,1728]{0,1:T(8,128)(2,1)} async-done(((bf16[2048,1728]{0,1:T(8,128)(2,1)}), bf16[1024,1728]{0,1:T(8,128)(2,1)}) %reduce-scatter.9.cloned.1.call-update) | async-done | bytes 3538960 | tf_op jit(solution)/shard_map/reduce_scatter | solution.py:84
  681.6 2.8 convert_element_type.56
  684.4 2.4 fusion
  686.8 0.0 all-gather.8.cloned.1.call-update
  686.8 0.0 reduce-scatter.11.cloned.1.call-start
  686.9 49.5 %all-gather.8.cloned.1.call-done = bf16[2048,864]{0,1:T(8,128)(2,1)} async-done(((bf16[1024,864]{0,1:T(8,128)(2,1)}), bf16[2048,864]{0,1:T(8,128)(2,1)}) %all-gather.8.cloned.1.call-update) | async-done | bytes 3538960 | tf_op jit(solution)/shard_map/all_gather | solution.py:92
  736.3 16.5 %convolution_convert_fusion = bf16[2048,2560]{1,0:T(8,128)(2,1)} fusion(bf16[2048,864]{0,1:T(8,128)(2,1)} %all-gather.8.cloned.1.call-done, bf16[864,2560]{1,0:T(8,128)(2,1)} %param.17), kind=kOutput, calls=%fused_computation | convolution fusion | flops 9064939520 | bytes 18448384 | tf_op jit(solution)/shard_map/dot_general | solution.py:91
  752.8 0.0 reduce-scatter.11.cloned.1.call-update
  752.8 119.6 %reduce-scatter.11.cloned.1.call-done = bf16[128,2560]{1,0:T(8,128)(2,1)} async-done(((bf16[2048,2560]{1,0:T(8,128)(2,1)}), bf16[128,2560]{1,0:T(8,128)(2,1)}) %reduce-scatter.11.cloned.1.call-update) | async-done | bytes 655376 | tf_op jit(solution)/shard_map/reduce_scatter | solution.py:96
  872.5 0.0 copy-done.1
  872.5 2.3 convert_add_fusion
  (5 shorter events, 0.0 us)
Async XLA Ops:
  6.5 287.5 %reduce-scatter.5.cloned.1.call-start = ((), (), s32[]{:S(2)}) async-start(), calls=%async_computation.4 | async-start | bytes 10616832 | tf_op jit(solution)/shard_map/reduce_scatter | solution.py:61
  15.5 15.7 %collective-permute-start = (bf16[1,128,2560]{2,1,0:T(8,128)(2,1)S(1)}, bf16[1,128,2560]{2,1,0:T(8,128)(2,1)S(1)}, u32[]{:S(2)}, u32[]{:S(2)}) collective-permute-start(bf16[1,128,2560]{2,1,0:T(8,128)(2,1)S(1)} %get-tuple-element.6), channel_id=1, source_target_pairs={{0,2},{2,0},{4,6},{6,4},{8,10},{10,8},{12,14},{14,12},{1,3},{3,1},... | collective-permute-start | bytes 1966088 | tf_op jit(solution)/shard_map/ppermute | solution.py:21
  32.6 29.0 %collective-permute-start.1 = (bf16[2,128,2560]{2,1,0:T(8,128)(2,1)}, bf16[2,128,2560]{2,1,0:T(8,128)(2,1)S(1)}, u32[]{:S(2)}, u32[]{:S(2)}) collective-permute-start(bf16[2,128,2560]{2,1,0:T(8,128)(2,1)} %get-tuple-element.8), channel_id=1, source_target_pairs={{0,4},{2,6},{4,0},{6,2},{8,12},{10,14},{12,8},{14,10},{1,5},{3,7},... | collective-permute-start | bytes 3932168 | tf_op jit(solution)/shard_map/ppermute | solution.py:21
  62.3 113.3 %collective-permute-start.2 = (bf16[4,128,2560]{2,1,0:T(8,128)(2,1)S(1)}, bf16[4,128,2560]{2,1,0:T(8,128)(2,1)}, u32[]{:S(2)}, u32[]{:S(2)}) collective-permute-start(bf16[4,128,2560]{2,1,0:T(8,128)(2,1)S(1)} %bitcast.26), channel_id=1, source_target_pairs={{0,8},{2,10},{4,12},{6,14},{8,0},{10,2},{12,4},{14,6},{1,9},{3,11}... | collective-permute-start | bytes 7864328 | tf_op jit(solution)/shard_map/ppermute | solution.py:21
  177.8 13.1 %slice-start = ((s8[8847360]{0:T(1024)(128)(4,1)}), s8[458752]{0:T(1024)(128)(4,1)S(1)}, s32[]{:S(2)}) async-start(s8[8847360]{0:T(1024)(128)(4,1)} %bitcast.32), calls=%async_computation.11 | async-start | bytes 917504
  178.8 12.0 %slice-start.1 = ((s8[8847360]{0:T(1024)(128)(4,1)}), s8[4194304]{0:T(1024)(128)(4,1)S(1)}, s32[]{:S(2)}) async-start(s8[8847360]{0:T(1024)(128)(4,1)} %bitcast.32), calls=%async_computation.12 | async-start | bytes 8388608
  178.9 12.0 %slice-start.2 = ((s8[8847360]{0:T(1024)(128)(4,1)}), s8[4194304]{0:T(1024)(128)(4,1)S(1)}, s32[]{:S(2)}) async-start(s8[8847360]{0:T(1024)(128)(4,1)} %bitcast.32), calls=%async_computation.13 | async-start | bytes 8388608
  207.4 141.6 %all-gather.4.cloned.1.call-start = ((), (), s32[]{:S(2)}) async-start(), calls=%async_computation.5 | async-start | bytes 5308416 | tf_op jit(solution)/shard_map/all_gather | solution.py:69
  299.5 167.7 %reduce-scatter.7.cloned.1.call-start = ((), (), s32[]{:S(2)}) async-start(), calls=%async_computation.6 | async-start | bytes 5898240 | tf_op jit(solution)/shard_map/reduce_scatter | solution.py:73
  364.0 103.2 %copy-start = (f32[128,2560]{1,0:T(8,128)S(1)}, f32[128,2560]{1,0:T(8,128)}, u32[]{:S(2)}) copy-start(f32[128,2560]{1,0:T(8,128)} %param.9) | copy-start | bytes 3932164
  364.0 109.5 %copy-start.2 = (f32[2560]{0:T(1024)S(1)}, f32[2560]{0:T(1024)}, u32[]{:S(2)}) copy-start(f32[2560]{0:T(1024)} %param.14) | copy-start | bytes 30724
  364.0 198.9 %all-gather.6.cloned.1.call-start = ((), (), s32[]{:S(2)}) async-start(), calls=%async_computation.7 | async-start | bytes 11141120 | tf_op jit(solution)/shard_map/all_gather | solution.py:79
  475.6 205.9 %reduce-scatter.9.cloned.1.call-start = ((), (), s32[]{:S(2)}) async-start(), calls=%async_computation.8 | async-start | bytes 10616832 | tf_op jit(solution)/shard_map/reduce_scatter | solution.py:84
  562.9 14.8 %copy-start.3 = (bf16[2048,2560]{1,0:T(8,128)(2,1)S(1)}, bf16[2048,2560]{1,0:T(8,128)(2,1)}, u32[]{:S(2)}) copy-start(bf16[2048,2560]{1,0:T(8,128)(2,1)} %all-gather.6.cloned.1.call-done) | copy-start | bytes 31457284
  597.5 138.8 %all-gather.8.cloned.1.call-start = ((), (), s32[]{:S(2)}) async-start(), calls=%async_computation.9 | async-start | bytes 5308416 | tf_op jit(solution)/shard_map/all_gather | solution.py:92
  686.8 185.7 %reduce-scatter.11.cloned.1.call-start = ((), (), s32[]{:S(2)}) async-start(), calls=%async_computation.10 | async-start | bytes 11141120 | tf_op jit(solution)/shard_map/reduce_scatter | solution.py:96
  752.8 119.7 %copy-start.1 = (bf16[128,2560]{1,0:T(8,128)(2,1)S(1)}, bf16[128,2560]{1,0:T(8,128)(2,1)}, u32[]{:S(2)}) copy-start(bf16[128,2560]{1,0:T(8,128)(2,1)} %reduce-scatter.7.cloned.1.call-done) | copy-start | bytes 1966084
Sparse Core Ops, SparseCore 0:
  207.5 86.4 reduce-scatter.4
  299.6 49.3 all-gather.3
  364.2 102.9 reduce-scatter.6
  475.8 87.1 all-gather.5
  597.6 83.9 reduce-scatter.8
  686.9 49.3 all-gather.7
  753.0 119.4 reduce-scatter.10
